TPU v7x, 32 devices: a whole 2x2x4 slice. The times are simulated.
32 devices in a mesh: dp: 4 (over y, core), mp: 8 (over z, x).
Axes of the slice: x: 2, y: 2, z: 4, core: 2. Of those that a mesh axis runs over, the one named last changes fastest.
Arguments:
- pair_tokens: bfloat16 [64, 48, 8192], P('dp', None, 'mp'), may hold values from -6 to 6
- norm_gain: float32 [8192], replicated, may hold values from 0.1 to 1.9
- q_weight: bfloat16 [8192, 4096], P('dp', 'mp'), may hold values from -1.5 to 1.5
- k_weight: bfloat16 [8192, 1024], P('dp', 'mp'), may hold values from -1.5 to 1.5
- value_weight: bfloat16 [8192, 1024], P('dp', 'mp'), may hold values from -0.0625 to 0.0625
- o_weight: bfloat16 [4096, 8192], P('mp', 'dp'), may hold values from -0.375 to 0.375
- pair_row: int32 [64], replicated, may hold values from 0 to 15, as said below
- pair_span: int32 [64, 2], replicated, may hold values from 0 to 128, as said below
- block_ids: int32 [2048], P('dp'), may hold values from 0 to 11, as said below
Outputs:
- attn_out: bfloat16 [2048, 8192], P('dp', 'mp')
Inputs may be any that keep to these rules, and one draw needn't show every extreme that they name: `pair_row`: every packed row is tiled exactly by the spans of the pairs that name it; the pairs listed on one index of dp that name rows of one index of dp number at most 4, and 4 is reached. `pair_span`: each span holds one pair, start before end; end - start is at least 3 and at most 48; 48 is reached in every row, and the last pair of every row ends at 128. `block_ids`: the pair's place counts the pairs of its row in order of position; roles are 0 prompt, 1 chosen, 2 rejected, in that order within each pair, each present; consistent with pair_row and pair_span.
All inputs are finite; a program needn't handle non-finite values.
Results may differ from a plain program's by a relative error of at most 0.013.
Values may be sent and summed in bfloat16 or wider, within the bound.
A program may use at most 128 MiB of HBM per device.

v0:
```python
import jax
import jax.numpy as jnp
from jax import lax
from jax.sharding import PartitionSpec as P

HEAD_SIZE = 128
ROW_TOKENS = 128
QUERY_PER_KV = 4


def apply_rotary(values, token_position, heads):
    half = HEAD_SIZE // 2
    freq = 500000.0 ** (-(jnp.arange(half, dtype=jnp.float32) * 2.0 / HEAD_SIZE))
    angle = token_position.astype(jnp.float32)[:, None] * freq[None, :]
    cosine = jnp.cos(angle)[:, None, :]
    sine = jnp.sin(angle)[:, None, :]
    shaped = values.reshape(values.shape[0], heads, HEAD_SIZE)
    first = shaped[..., :half]
    second = shaped[..., half:]
    turned = jnp.concatenate(
        [first * cosine - second * sine, second * cosine + first * sine], axis=-1
    )
    return turned.reshape(values.shape[0], heads * HEAD_SIZE).astype(jnp.bfloat16)


def row_mask(ids):
    pair_of = ids // 3
    role_of = ids % 3
    steps_a = jnp.arange(ids.shape[0])
    causal = steps_a[None, :] <= steps_a[:, None]
    same = pair_of[:, None] == pair_of[None, :]
    hidden_pair = (role_of[:, None] == 2) & (role_of[None, :] == 1)
    return causal & same & jnp.logical_not(hidden_pair)


def local(
    pair_tokens,
    norm_gain,
    q_weight,
    k_weight,
    value_weight,
    o_weight,
    pair_row,
    pair_span,
    block_ids,
):
    dp_count = lax.axis_size("dp")
    own_index = lax.axis_index("dp")
    pairs_dev = pair_tokens.shape[0]
    pair_cap = pair_tokens.shape[1]
    width_local = pair_tokens.shape[2]
    all_pairs = pair_row.shape[0]
    most_sent = -(-pairs_dev // dp_count)
    tok_dev = block_ids.shape[0]
    rows_dev = tok_dev // ROW_TOKENS
    owners_all = (pair_row // rows_dev).reshape(dp_count, pairs_dev)
    same_owner = owners_all[:, :, None] == owners_all[:, None, :]
    listed = jnp.arange(pairs_dev)
    before = listed[None, :] < listed[:, None]
    rank_all = jnp.sum((same_owner & before[None]).astype(jnp.int32), axis=2)
    own_owner = lax.dynamic_index_in_dim(owners_all, own_index, 0, keepdims=False)
    own_rank = lax.dynamic_index_in_dim(rank_all, own_index, 0, keepdims=False)
    outgoing = jnp.zeros((dp_count * most_sent, pair_cap, width_local), jnp.bfloat16)
    outgoing = outgoing.at[own_owner * most_sent + own_rank].set(pair_tokens)
    incoming = lax.all_to_all(
        outgoing.reshape(dp_count, most_sent * pair_cap, width_local),
        "dp",
        split_axis=0,
        concat_axis=0,
        tiled=True,
    )
    slots = jnp.arange(pair_cap, dtype=jnp.int32)
    length = pair_span[:, 1] - pair_span[:, 0]
    source = jnp.arange(all_pairs, dtype=jnp.int32) // pairs_dev
    target = (pair_row % rows_dev)[:, None] * ROW_TOKENS + pair_span[:, 0][:, None] + slots[None, :]
    usable = (owners_all.reshape(-1) == own_index)[:, None] & (slots[None, :] < length[:, None])
    slot_index = (source * most_sent + rank_all.reshape(-1))[:, None] * pair_cap + slots[None, :]
    buffer_size = dp_count * most_sent * pair_cap
    slot_index = jnp.where(usable, slot_index, buffer_size)
    placement_map = jnp.full((buffer_size,), tok_dev, jnp.int32)
    placement_map = placement_map.at[slot_index.reshape(-1)].set(target.reshape(-1), mode="drop")
    packed_local = jnp.zeros((tok_dev, width_local), jnp.bfloat16)
    packed_local = packed_local.at[placement_map].set(
        incoming.reshape(buffer_size, width_local), mode="drop"
    )
    packed = lax.all_gather(packed_local, "mp", axis=1, tiled=True)
    wide = packed.astype(jnp.float32)
    scale = lax.rsqrt(jnp.mean(wide * wide, axis=-1, keepdims=True) + 1e-05)
    normed = (wide * scale * norm_gain[None, :]).astype(jnp.bfloat16)

    def add_rows(piece):
        return jnp.dot(normed, piece, preferred_element_type=jnp.float32)

    query_heads = add_rows(lax.all_gather(q_weight, "dp", axis=0, tiled=True))
    key_rows = add_rows(lax.all_gather(k_weight, "dp", axis=0, tiled=True))
    value_sum = add_rows(lax.all_gather(value_weight, "dp", axis=0, tiled=True))
    value_heads = value_sum.astype(jnp.bfloat16)
    ids_rows = block_ids.reshape(rows_dev, ROW_TOKENS)
    visible = jax.vmap(row_mask)(ids_rows)
    token_position = (jnp.sum(visible.astype(jnp.int32), axis=2) - 1).reshape(tok_dev)
    kv_local = k_weight.shape[1] // HEAD_SIZE
    q_local = q_weight.shape[1] // HEAD_SIZE
    rotated_query = apply_rotary(query_heads, token_position, q_local).reshape(
        rows_dev, ROW_TOKENS, kv_local, QUERY_PER_KV, HEAD_SIZE
    )
    rotated_key = apply_rotary(key_rows, token_position, kv_local).reshape(
        rows_dev, ROW_TOKENS, kv_local, HEAD_SIZE
    )
    v_rows = value_heads.reshape(rows_dev, ROW_TOKENS, kv_local, HEAD_SIZE)
    scores = jnp.einsum(
        "rihgd,rjhd->rhgij", rotated_query, rotated_key, preferred_element_type=jnp.float32
    ) * HEAD_SIZE ** (-0.5)
    scores = jnp.where(visible[:, None, None], scores, -1e30)
    top = jnp.max(scores, axis=-1, keepdims=True)
    expo = jnp.exp(scores - top)
    probs = (expo / jnp.sum(expo, axis=-1, keepdims=True)).astype(jnp.bfloat16)
    attn = jnp.einsum(
        "rhgij,rjhd->rihgd", probs, v_rows, preferred_element_type=jnp.float32
    ).astype(jnp.bfloat16)
    attn = attn.reshape(tok_dev, q_local * HEAD_SIZE)
    terms = jnp.dot(
        attn, lax.all_gather(o_weight, "dp", axis=1, tiled=True), preferred_element_type=jnp.float32
    )
    return lax.psum_scatter(terms.astype(jnp.bfloat16), "mp", scatter_dimension=1, tiled=True)


def solution(mesh):
    placed = (
        P("dp", None, "mp"),
        P(),
        P("dp", "mp"),
        P("dp", "mp"),
        P("dp", "mp"),
        P("mp", "dp"),
        P(),
        P(),
        P("dp"),
    )
    return jax.shard_map(
        local, mesh=mesh, in_specs=placed, out_specs=P("dp", "mp"), check_vma=False
    )
```

profile of v0, /device:TPU:0, one launch (start us, length us, event | category | flops | bytes accessed | tf_op | source)
XLA Modules:
  0.0 501.9 jit_solution(16550077983021786801)
XLA Ops:
  6.5 0.0 copy-start.1
  6.5 0.0 copy-start.2
  6.6 0.7 broadcast_compare_fusion.2
  7.3 0.1 eq.64
  7.4 0.2 convert_reduce_fusion.1
  7.6 0.0 copy-start
  7.6 1.3 broadcast_in_dim.24
  8.9 5.4 %scatter_fusion = bf16[16,48,1024]{2,1,0:T(8,128)(2,1)} fusion(bf16[16,48,1024]{2,1,0:T(8,128)(2,1)} %broadcast_in_dim.24, s32[16]{0:T(128)S(1)} %fusion.33, bf16[16,48,1024]{2,1,0:T(8,128)(2,1)} %param.9), kind=kCustom, calls=%fused_computation.1 | custom fusion | bytes 4718656 | tf_op jit(solution)/shard_map/scatter | solution.py:64
  14.4 4.3 all-to-all-start
  18.6 0.0 copy-start.3
  18.6 0.0 all-gather.6.cloned.1.call-start
  18.6 0.1 reshape.394
  18.7 0.0 copy-done.1
  18.7 0.0 copy-done.2
  18.7 0.1 add_select_fusion
  18.8 0.1 select_n.97
  18.9 0.1 iota_add_fusion
  19.0 0.1 reshape.406
  19.1 11.8 %scatter_custom_fusion = s32[768]{0:T(1024)S(1)} fusion(s32[3072]{0:T(1024)S(1)} %bitcast.87, s32[3072]{0:T(1024)S(1)} %reshape.406, s32[]{:T(128)} %constant.90.clone.1), kind=kCustom, calls=%fused_computation.60 | custom fusion | bytes 3076 | tf_op jit(solution)/shard_map/scatter | solution.py:81
  30.9 7.8 %all-to-all-done = bf16[4,192,1024]{2,1,0:T(8,128)(2,1)S(1)} async-done(((bf16[4,192,1024]{2,1,0:T(8,128)(2,1)}), bf16[4,192,1024]{2,1,0:T(8,128)(2,1)S(1)}, u32[]{:S(2)}, u32[]{:S(2)}) %all-to-all-start) | async-done | bytes 1572896 | tf_op jit(solution)/shard_map/all_to_all | solution.py:65
  38.7 6.7 %scatter_custom_fusion.2 = bf16[512,1024]{1,0:T(8,128)(2,1)} fusion(s32[768]{0:T(1024)S(1)} %compare_select_fusion.1, bf16[768,1024]{1,0:T(8,128)(2,1)S(1)} %bitcast.83, bf16[]{:T(256)} %constant.89.clone.1), kind=kCustom, calls=%fused_computation.26 | custom fusion | bytes 1048578 | tf_op jit(solution)/shard_map/scatter | solution.py:83
  45.3 0.0 all-gather.6.cloned.1.call-update
  45.3 0.0 all-gather.12.cloned.1.call-start
  45.4 0.7 all-gather.12.cloned.1.call-update
  46.1 0.0 all-gather.10.cloned.1.call-start
  46.1 0.7 all-gather.10.cloned.1.call-update
  46.8 0.0 all-gather.8.cloned.1.call-start
  46.9 0.5 all-gather.8.cloned.1.call-update
  47.4 0.0 all-gather.14.cloned.1.call-start
  47.5 0.5 all-gather.14.cloned.1.call-update
  48.0 0.0 reduce-scatter.2.cloned.1.call-start
  48.1 0.0 copy-done
  48.1 0.2 convert_reduce_fusion
  48.4 1.0 multiply_cosine_fusion
  49.4 121.7 %all-gather.6.cloned.1.call-done = bf16[512,8192]{1,0:T(8,128)(2,1)} async-done(((bf16[512,1024]{1,0:T(8,128)(2,1)}), bf16[512,8192]{1,0:T(8,128)(2,1)}) %all-gather.6.cloned.1.call-update) | async-done | bytes 8388624 | tf_op jit(solution)/shard_map/all_gather | solution.py:86
  171.0 5.1 %fusion = f32[512]{0:T(512)S(1)} fusion(bf16[512,8192]{1,0:T(8,128)(2,1)} %all-gather.6.cloned.1.call-done), kind=kLoop, calls=%fused_computation.5 | loop fusion | flops 12582400 | bytes 8390656 | tf_op jit(solution)/shard_map/reduce_sum | solution.py:88
  176.1 52.9 %all-gather.12.cloned.1.call-done = bf16[8192,512]{1,0:T(8,128)(2,1)} async-done(((bf16[2048,512]{1,0:T(8,128)(2,1)}), bf16[8192,512]{1,0:T(8,128)(2,1)}) %all-gather.12.cloned.1.call-update) | async-done | bytes 8388624 | tf_op jit(solution)/shard_map/all_gather | solution.py:94
  229.0 0.0 copy-done.3
  229.0 11.4 %fusion.35 = f32[512,512]{0,1:T(8,128)S(1)} fusion(bf16[8192,512]{1,0:T(8,128)(2,1)} %all-gather.12.cloned.1.call-done, bf16[512,8192]{1,0:T(8,128)(2,1)} %all-gather.6.cloned.1.call-done, f32[8192]{0:T(1024)S(1)} %copy-done.3, f32[512]{0:T(512)S(1)} %add_rsqrt_fusion), kind=kOutput, calls=%fused_computation.87 | convolution fusion | flops 4311744512 | bytes 17860608 | tf_op jit(solution)/shard_map/dot_general | solution.py:92
  240.4 0.1 fusion.39
  240.5 0.3 copy.33
  240.8 0.3 copy.34
  241.2 12.1 %all-gather.10.cloned.1.call-done = bf16[8192,128]{1,0:T(8,128)(2,1)} async-done(((bf16[2048,128]{1,0:T(8,128)(2,1)}), bf16[8192,128]{1,0:T(8,128)(2,1)}) %all-gather.10.cloned.1.call-update) | async-done | bytes 2097168 | tf_op jit(solution)/shard_map/all_gather | solution.py:95
  253.2 6.5 %convolution_bitcast_fusion = f32[512,1,128]{0,2,1:T(8,128)S(1)} fusion(bf16[8192,128]{1,0:T(8,128)(2,1)} %all-gather.10.cloned.1.call-done, bf16[512,8192]{1,0:T(8,128)(2,1)} %all-gather.6.cloned.1.call-done, f32[8192]{0:T(1024)S(1)} %copy-done.3, f32[512]{0:T(512)S(1)} %add_rsqrt_fusion), kind=kOutput, calls=%fused_computation.14 | convolution fusion | flops 1090519040 | bytes 10782720 | tf_op jit(solution)/shard_map/dot_general | solution.py:92
  259.7 0.6 fusion.18
  260.3 0.1 copy.32
  260.4 0.3 subtract_convert_fusion
  260.7 0.3 pad_maximum_fusion
  261.0 0.3 fusion.40
  261.4 0.2 fusion.6
  261.5 15.7 %all-gather.8.cloned.1.call-done = bf16[8192,128]{1,0:T(8,128)(2,1)} async-done(((bf16[2048,128]{1,0:T(8,128)(2,1)}), bf16[8192,128]{1,0:T(8,128)(2,1)}) %all-gather.8.cloned.1.call-update) | async-done | bytes 2097168 | tf_op jit(solution)/shard_map/all_gather | solution.py:96
  277.2 6.4 %convolution_convert_fusion.2 = bf16[512,128]{1,0:T(8,128)(2,1)S(1)} fusion(bf16[8192,128]{1,0:T(8,128)(2,1)} %all-gather.8.cloned.1.call-done, bf16[512,8192]{1,0:T(8,128)(2,1)} %all-gather.6.cloned.1.call-done, f32[8192]{0:T(1024)S(1)} %copy-done.3, f32[512]{0:T(512)S(1)} %add_rsqrt_fusion), kind=kOutput, calls=%fused_computation.15 | convolution fusion | flops 1090584576 | bytes 10651648 | tf_op jit(solution)/shard_map/dot_general | solution.py:92
  283.6 0.4 fusion.5
  283.9 0.3 copy.26
  284.3 52.7 %all-gather.14.cloned.1.call-done = bf16[512,8192]{1,0:T(8,128)(2,1)} async-done(((bf16[512,2048]{1,0:T(8,128)(2,1)}), bf16[512,8192]{1,0:T(8,128)(2,1)}) %all-gather.14.cloned.1.call-update) | async-done | bytes 8388624 | tf_op jit(solution)/shard_map/all_gather | solution.py:122
  336.9 10.1 %convolution_convert_fusion = bf16[512,8192]{1,0:T(8,128)(2,1)} fusion(bf16[512,8192]{1,0:T(8,128)(2,1)} %all-gather.14.cloned.1.call-done, bf16[64,8,4,128]{3,2,1,0:T(4,128)(2,1)S(1)} %bitcast.86), kind=kOutput, calls=%fused_computation.8 | convolution fusion | flops 4299161600 | bytes 17301504 | tf_op jit(solution)/shard_map/dot_general | solution.py:121
  347.0 0.0 reduce-scatter.2.cloned.1.call-update
  347.0 148.0 %reduce-scatter.2.cloned.1.call-done = bf16[512,1024]{1,0:T(8,128)(2,1)} async-done(((bf16[512,8192]{1,0:T(8,128)(2,1)}), bf16[512,1024]{1,0:T(8,128)(2,1)}) %reduce-scatter.2.cloned.1.call-update) | async-done | bytes 1048592 | tf_op jit(solution)/shard_map/reduce_scatter | solution.py:124
  (13 shorter events, 0.1 us)
Async XLA Ops:
  6.5 12.2 %copy-start.1 = (s32[64]{0:T(128)S(1)}, s32[64]{0:T(128)}, u32[]{:S(2)}) copy-start(s32[64]{0:T(128)} %param.15) | copy-start | bytes 772
  6.5 12.2 %copy-start.2 = (s32[64,2]{0,1:T(2,128)S(1)}, s32[64,2]{0,1:T(2,128)}, u32[]{:S(2)}) copy-start(s32[64,2]{0,1:T(2,128)} %param.16) | copy-start | bytes 1540
  7.6 40.5 %copy-start = (s32[512]{0:T(512)S(1)}, s32[512]{0:T(512)}, u32[]{:S(2)}) copy-start(s32[512]{0:T(512)} %param.17) | copy-start | bytes 6148
  14.4 24.3 %all-to-all-start = ((bf16[4,192,1024]{2,1,0:T(8,128)(2,1)}), bf16[4,192,1024]{2,1,0:T(8,128)(2,1)S(1)}, u32[]{:S(2)}, u32[]{:S(2)}) async-start(bf16[4,192,1024]{2,1,0:T(8,128)(2,1)} %bitcast.6), calls=%async_computation | async-start | bytes 3145728 | tf_op jit(solution)/shard_map/all_to_all | solution.py:65
  18.6 210.4 %copy-start.3 = (f32[8192]{0:T(1024)S(1)}, f32[8192]{0:T(1024)}, u32[]{:S(2)}) copy-start(f32[8192]{0:T(1024)} %param.10) | copy-start | bytes 98308
  18.6 152.4 %all-gather.6.cloned.1.call-start = ((), (), s32[]{:S(2)}) async-start(), calls=%async_computation.2 | async-start | bytes 9437184 | tf_op jit(solution)/shard_map/all_gather | solution.py:86
  45.3 183.7 %all-gather.12.cloned.1.call-start = ((), (), s32[]{:S(2)}) async-start(), calls=%async_computation.5 | async-start | bytes 10485760 | tf_op jit(solution)/shard_map/all_gather | solution.py:94
  46.1 207.1 %all-gather.10.cloned.1.call-start = ((), (), s32[]{:S(2)}) async-start(), calls=%async_computation.4 | async-start | bytes 2621440 | tf_op jit(solution)/shard_map/all_gather | solution.py:95
  46.8 230.4 %all-gather.8.cloned.1.call-start = ((), (), s32[]{:S(2)}) async-start(), calls=%async_computation.3 | async-start | bytes 2621440 | tf_op jit(solution)/shard_map/all_gather | solution.py:96
  47.4 289.5 %all-gather.14.cloned.1.call-start = ((), (), s32[]{:S(2)}) async-start(), calls=%async_computation.6 | async-start | bytes 10485760 | tf_op jit(solution)/shard_map/all_gather | solution.py:122
  48.0 447.0 %reduce-scatter.2.cloned.1.call-start = ((), (), s32[]{:S(2)}) async-start(), calls=%async_computation.7 | async-start | bytes 9437184 | tf_op jit(solution)/shard_map/reduce_scatter | solution.py:124
Sparse Core Ops, SparseCore 0:
  45.5 125.4 all-gather.5
  172.6 56.4 all-gather.11
  230.6 22.5 all-gather.9
  254.7 22.5 all-gather.7
  278.6 58.2 all-gather.13
  347.2 147.8 reduce-scatter.1
where the time goes:
time: 502 us
  waiting for transfers between devices  413 us (82%)
  matrix products  35 us (7%)
  local copies, waits for them, and re-layouts  26.7 us (5%)
  between operations  13.7 us (3%)
  other arithmetic  8.88 us (2%)
    reduce_scatter x1, waiting for transfers between devices, local(): lax.psum_scatter(terms.astype(jnp.bfloat16), 'mp', scatter_dimension=1, t...  148 us
    all_gather x1, waiting for transfers between devices, local(): packed = lax.all_gather(packed_local, 'mp', axis=1, tiled=True)  122 us
    all_gather x1, waiting for transfers between devices, local(): query_heads = add_rows(lax.all_gather(q_weight, 'dp', axis=0, tiled=True))  52.9 us
    all_gather x1, waiting for transfers between devices, local(): lax.all_gather(o_weight, 'dp', axis=1, tiled=True)  52.7 us
    dot_general x3, matrix products, add_rows(): return jnp.dot(normed, piece, preferred_element_type=jnp.float32)  24.2 us
    all_gather x1, waiting for transfers between devices, local(): value_sum = add_rows(lax.all_gather(value_weight, 'dp', axis=0, tiled=True))  15.7 us
    all_gather x1, waiting for transfers between devices, local(): key_rows = add_rows(lax.all_gather(k_weight, 'dp', axis=0, tiled=True))  12.1 us
    scatter x1, local copies, waits for them, and re-layouts, local(): placement_map.at[slot_index.reshape(-1)]  11.8 us
  transfers between devices with their start and end apart: 7, of which 7 were waited for; matrix products, arithmetic and copies ran while one was open for 9% of the time, Pallas kernels for 0%

commit v1 on v0

--- a/solution.py
+++ b/solution.py
@@ -83,7 +83,12 @@
     packed_local = packed_local.at[placement_map].set(
         incoming.reshape(buffer_size, width_local), mode="drop"
     )
-    packed = lax.all_gather(packed_local, "mp", axis=1, tiled=True)
+    ring = [packed_local]
+    for hop in range(7):
+        ring.append(lax.ppermute(ring[-1], "mp", [(dev, (dev + 1) % 8) for dev in range(8)]))
+    packed = jnp.roll(
+        jnp.concatenate(ring[::-1], axis=1), (lax.axis_index("mp") + 1) * ring[0].shape[1], axis=1
+    )
     wide = packed.astype(jnp.float32)
     scale = lax.rsqrt(jnp.mean(wide * wide, axis=-1, keepdims=True) + 1e-05)
     normed = (wide * scale * norm_gain[None, :]).astype(jnp.bfloat16)

time: 502 us -> 444 us (0.88)
  waiting for transfers between devices: 413 us -> 334 us
  local copies, waits for them, and re-layouts: 26.7 us -> 44.8 us
    ppermute x0 -> x7, waiting for transfers between devices: none -> 171 us  [local(): lax.ppermute(ring[-1], 'mp', [(dev, (dev + 1) % 8) for dev in range(8)])]
    all_gather x1 -> x0, waiting for transfers between devices: 122 us -> none  [local(): packed = lax.all_gather(packed_local, 'mp', axis=1, tiled=True)]
    all_gather x1, waiting for transfers between devices: 52.9 us -> 0.01 us  [local(): query_heads = add_rows(lax.all_gather(q_weight, 'dp', axis=0, tiled=True))]
    all_gather x1, waiting for transfers between devices: 52.7 us -> 0.02 us  [local(): lax.all_gather(o_weight, 'dp', axis=1, tiled=True)]
    unnamed x10 -> x35, local copies, waits for them, and re-layouts: 0.68 us -> 19.3 us
    all_gather x1, waiting for transfers between devices: 15.7 us -> 0.02 us  [local(): value_sum = add_rows(lax.all_gather(value_weight, 'dp', axis=0, tiled=True))]
    all_gather x1, waiting for transfers between devices: 12.1 us -> 0.02 us  [local(): key_rows = add_rows(lax.all_gather(k_weight, 'dp', axis=0, tiled=True))]
    all_to_all x1, waiting for transfers between devices: 7.76 us -> 15.6 us  [local(): lax.all_to_all(outgoing.reshape(dp_count, most_sent * pair_cap, width_loc...]
  transfers between devices with their start and end apart: 7 -> 13, of which waited for: 7 -> 9; matrix products, arithmetic and copies ran while one was open for 9% -> 16% of each run, Pallas kernels for 0% -> 0%
where the time goes in v1:
time: 444 us
  waiting for transfers between devices  334 us (75%)
  local copies, waits for them, and re-layouts  44.8 us (10%)
  matrix products  36.8 us (8%)
  between operations  13.6 us (3%)
  other arithmetic  8.45 us (2%)
  starting transfers between devices  5.9 us (1%)
    ppermute x7, waiting for transfers between devices, local(): lax.ppermute(ring[-1], 'mp', [(dev, (dev + 1) % 8) for dev in range(8)])  171 us
    reduce_scatter x1, waiting for transfers between devices, local(): lax.psum_scatter(terms.astype(jnp.bfloat16), 'mp', scatter_dimension=1, t...  145 us
    dot_general x3, matrix products, add_rows(): return jnp.dot(normed, piece, preferred_element_type=jnp.float32)  25.1 us
    unnamed x35, local copies, waits for them, and re-layouts  19.3 us
    all_to_all x1, waiting for transfers between devices, local(): lax.all_to_all(outgoing.reshape(dp_count, most_sent * pair_cap, width_loc...  15.6 us
    scatter x1, local copies, waits for them, and re-layouts, local(): placement_map.at[slot_index.reshape(-1)]  11.8 us
    dot_general x1, matrix products, local(): jnp.dot(attn, lax.all_gather(o_weight, 'dp', axis=1, tiled=True), preferr...  10.1 us
  transfers between devices with their start and end apart: 13, of which 9 were waited for; matrix products, arithmetic and copies ran while one was open for 16% of the time, Pallas kernels for 0%

profile of v1, /device:TPU:0, one launch (start us, length us, event | category | flops | bytes accessed | tf_op | source)
XLA Modules:
  0.0 443.7 jit_solution(17201823302153776601)
XLA Ops:
  6.5 0.7 all-gather.7.cloned.1.call-update
  7.3 0.7 all-gather.5.cloned.1.call-update
  8.1 0.7 all-gather.9.cloned.1.call-update
  8.7 0.7 broadcast_compare_fusion.2
  9.5 0.2 convert_reduce_fusion.1
  9.7 1.4 broadcast_in_dim.24
  11.2 5.5 %scatter_fusion = bf16[16,48,1024]{2,1,0:T(8,128)(2,1)} fusion(bf16[16,48,1024]{2,1,0:T(8,128)(2,1)} %broadcast_in_dim.24, s32[16]{0:T(128)S(1)} %fusion.35, bf16[16,48,1024]{2,1,0:T(8,128)(2,1)} %param.9), kind=kCustom, calls=%fused_computation.1 | custom fusion | bytes 4718656 | tf_op jit(solution)/shard_map/scatter | solution.py:64
  16.6 4.2 all-to-all-start
  20.9 0.1 reshape.394
  21.0 0.8 fusion.36
  21.8 0.1 add_select_fusion
  21.8 0.1 select_n.109
  22.1 11.8 %scatter_custom_fusion = s32[768]{0:T(1024)S(1)} fusion(s32[3072]{0:T(1024)S(1)} %bitcast.87, s32[3072]{0:T(1024)S(1)} %reshape.406, s32[]{:T(128)} %constant.112.clone.1), kind=kCustom, calls=%fused_computation.76 | custom fusion | bytes 3076 | tf_op jit(solution)/shard_map/scatter | solution.py:81
  33.9 15.6 %all-to-all-done = bf16[4,192,1024]{2,1,0:T(8,128)(2,1)S(1)} async-done(((bf16[4,192,1024]{2,1,0:T(8,128)(2,1)}), bf16[4,192,1024]{2,1,0:T(8,128)(2,1)S(1)}, u32[]{:S(2)}, u32[]{:S(2)}) %all-to-all-start) | async-done | bytes 1572896 | tf_op jit(solution)/shard_map/all_to_all | solution.py:65
  49.5 5.9 %scatter_custom_fusion.2 = bf16[512,1024]{1,0:T(8,128)(2,1)S(1)} fusion(s32[768]{0:T(1024)S(1)} %compare_select_fusion.1, bf16[768,1024]{1,0:T(8,128)(2,1)S(1)} %bitcast.83, bf16[]{:T(256)} %constant.111.clone.1), kind=kCustom, calls=%fused_computation.26 | custom fusion | bytes 1048578 | tf_op jit(solution)/shard_map/scatter | solution.py:83
  55.5 1.5 collective-permute-start
  57.0 26.2 %collective-permute-done = bf16[512,1024]{1,0:T(8,128)(2,1)S(1)} collective-permute-done((bf16[512,1024]{1,0:T(8,128)(2,1)S(1)}, bf16[512,1024]{1,0:T(8,128)(2,1)S(1)}, u32[]{:S(2)}, u32[]{:S(2)}) %collective-permute-start) | collective-permute-done | bytes 1048608 | tf_op jit(solution)/shard_map/ppermute | solution.py:88
  83.3 26.7 %collective-permute-done.1 = bf16[512,1024]{1,0:T(8,128)(2,1)S(1)} collective-permute-done((bf16[512,1024]{1,0:T(8,128)(2,1)S(1)}, bf16[512,1024]{1,0:T(8,128)(2,1)S(1)}, u32[]{:S(2)}, u32[]{:S(2)}) %collective-permute-start.1) | collective-permute-done | bytes 1048608 | tf_op jit(solution)/shard_map/ppermute | solution.py:88
  110.0 25.9 %collective-permute-done.2 = bf16[512,1024]{1,0:T(8,128)(2,1)S(1)} collective-permute-done((bf16[512,1024]{1,0:T(8,128)(2,1)S(1)}, bf16[512,1024]{1,0:T(8,128)(2,1)S(1)}, u32[]{:S(2)}, u32[]{:S(2)}) %collective-permute-start.2) | collective-permute-done | bytes 1048608 | tf_op jit(solution)/shard_map/ppermute | solution.py:88
  135.9 1.0 copy-done.1
  136.9 25.1 %collective-permute-done.3 = bf16[512,1024]{1,0:T(8,128)(2,1)S(1)} collective-permute-done((bf16[512,1024]{1,0:T(8,128)(2,1)S(1)}, bf16[512,1024]{1,0:T(8,128)(2,1)S(1)}, u32[]{:S(2)}, u32[]{:S(2)}) %collective-permute-start.3) | collective-permute-done | bytes 1048608 | tf_op jit(solution)/shard_map/ppermute | solution.py:88
  162.0 1.0 copy-done.3
  163.0 24.2 %collective-permute-done.4 = bf16[512,1024]{1,0:T(8,128)(2,1)S(1)} collective-permute-done((bf16[512,1024]{1,0:T(8,128)(2,1)S(1)}, bf16[512,1024]{1,0:T(8,128)(2,1)S(1)}, u32[]{:S(2)}, u32[]{:S(2)}) %collective-permute-start.4) | collective-permute-done | bytes 1048608 | tf_op jit(solution)/shard_map/ppermute | solution.py:88
  187.3 1.0 copy-done.5
  188.2 0.7 broadcast_compare_fusion.1
  188.9 22.8 %collective-permute-done.5 = bf16[512,1024]{1,0:T(8,128)(2,1)} collective-permute-done((bf16[512,1024]{1,0:T(8,128)(2,1)S(1)}, bf16[512,1024]{1,0:T(8,128)(2,1)}, u32[]{:S(2)}, u32[]{:S(2)}) %collective-permute-start.5) | collective-permute-done | bytes 1048608 | tf_op jit(solution)/shard_map/ppermute | solution.py:88
  211.8 0.8 add_select_fusion.2
  212.6 0.2 convert_reduce_fusion
  212.9 1.8 multiply_cosine_fusion
  214.6 19.9 %collective-permute-done.6 = bf16[512,1024]{1,0:T(8,128)(2,1)} collective-permute-done((bf16[512,1024]{1,0:T(8,128)(2,1)}, bf16[512,1024]{1,0:T(8,128)(2,1)}, u32[]{:S(2)}, u32[]{:S(2)}) %collective-permute-start.6) | collective-permute-done | bytes 1048608 | tf_op jit(solution)/shard_map/ppermute | solution.py:88
  234.5 1.3 constant_dynamic-update-slice_fusion.15
  235.9 1.3 constant_dynamic-update-slice_fusion.14
  237.2 1.3 constant_dynamic-update-slice_fusion.13
  238.5 1.3 constant_dynamic-update-slice_fusion.12
  239.8 1.3 constant_dynamic-update-slice_fusion.11
  241.2 0.1 constant_dynamic-update-slice_fusion.10
  241.3 0.1 constant_dynamic-update-slice_fusion.9
  241.3 0.1 constant_dynamic-update-slice_fusion.8
  241.4 1.3 constant_dynamic-update-slice_fusion.7
  242.8 1.3 constant_dynamic-update-slice_fusion.6
  244.1 0.1 constant_dynamic-update-slice_fusion.5
  244.2 0.1 constant_dynamic-update-slice_fusion.4
  244.3 0.1 constant_dynamic-update-slice_fusion.3
  244.4 0.1 constant_dynamic-update-slice_fusion.2
  244.5 0.1 constant_dynamic-update-slice_fusion.1
  244.6 0.1 constant_dynamic-update-slice_fusion
  244.7 5.7 %copy-done = bf16[512,16384]{1,0:T(8,128)(2,1)} copy-done((bf16[512,16384]{1,0:T(8,128)(2,1)}, bf16[512,16384]{1,0:T(8,128)(2,1)S(1)}, u32[]{:S(2)}) %copy-start) | copy-done | bytes 16777240
  250.4 1.7 fusion
  252.2 6.5 %convolution_bitcast_fusion = f32[512,1,128]{0,2,1:T(8,128)S(1)} fusion(bf16[8192,128]{1,0:T(8,128)(2,1)} %all-gather.7.cloned.1.call-done, f32[8192]{0:T(1024)S(1)} %copy-done.8, f32[512]{0:T(512)S(1)} %add_rsqrt_fusion, bf16[512,16384]{1,0:T(8,128)(2,1)} %copy-done, s32[]{:T(128)S(6)} %select_n.116), kind=kOutput, calls=%fused_computation.14 | convolution fusion | flops 1090519040 | bytes 10782724 | tf_op jit(solution)/shard_map/dot_general | solution.py:97
  258.7 0.6 fusion.18
  259.3 0.1 copy.32
  259.4 7.0 %convolution_convert_fusion.2 = bf16[512,128]{1,0:T(8,128)(2,1)} fusion(bf16[8192,128]{1,0:T(8,128)(2,1)} %all-gather.5.cloned.1.call-done, f32[8192]{0:T(1024)S(1)} %copy-done.8, f32[512]{0:T(512)S(1)} %add_rsqrt_fusion, bf16[512,16384]{1,0:T(8,128)(2,1)} %copy-done, s32[]{:T(128)S(6)} %select_n.116), kind=kOutput, calls=%fused_computation.15 | convolution fusion | flops 1090584576 | bytes 10651652 | tf_op jit(solution)/shard_map/dot_general | solution.py:97
  266.5 11.6 %fusion.37 = f32[512,512]{0,1:T(8,128)S(1)} fusion(bf16[8192,512]{1,0:T(8,128)(2,1)} %all-gather.9.cloned.1.call-done, f32[8192]{0:T(1024)S(1)} %copy-done.8, f32[512]{0:T(512)S(1)} %add_rsqrt_fusion, bf16[512,16384]{1,0:T(8,128)(2,1)} %copy-done, s32[]{:T(128)S(6)} %select_n.116), kind=kOutput, calls=%fused_computation.107 | convolution fusion | flops 4311744512 | bytes 17860612 | tf_op jit(solution)/shard_map/dot_general | solution.py:97
  278.1 0.1 fusion.41
  278.2 0.3 copy.33
  278.6 0.3 copy.34
  278.9 0.3 subtract_convert_fusion
  279.2 0.3 pad_maximum_fusion
  279.5 0.3 fusion.42
  279.8 0.2 fusion.6
  280.0 1.2 fusion.5
  281.2 0.3 copy.26
  281.6 10.1 %convolution_convert_fusion = bf16[512,8192]{1,0:T(8,128)(2,1)} fusion(bf16[512,8192]{1,0:T(8,128)(2,1)} %all-gather.11.cloned.1.call-done, bf16[64,8,4,128]{3,2,1,0:T(4,128)(2,1)S(1)} %bitcast.86), kind=kOutput, calls=%fused_computation.8 | convolution fusion | flops 4299161600 | bytes 17301504 | tf_op jit(solution)/shard_map/dot_general | solution.py:126
  291.7 145.5 %reduce-scatter.2.cloned.1.call-done = bf16[512,1024]{1,0:T(8,128)(2,1)} async-done(((bf16[512,8192]{1,0:T(8,128)(2,1)}), bf16[512,1024]{1,0:T(8,128)(2,1)}) %reduce-scatter.2.cloned.1.call-update) | async-done | bytes 1048592 | tf_op jit(solution)/shard_map/reduce_scatter | solution.py:129
  (44 shorter events, 0.6 us)
Async XLA Ops:
  6.5 245.6 %all-gather.7.cloned.1.call-start = ((), (), s32[]{:S(2)}) async-start(), calls=%async_computation.3 | async-start | bytes 2621440 | tf_op jit(solution)/shard_map/all_gather | solution.py:100
  7.3 252.2 %all-gather.5.cloned.1.call-start = ((), (), s32[]{:S(2)}) async-start(), calls=%async_computation.2 | async-start | bytes 2621440 | tf_op jit(solution)/shard_map/all_gather | solution.py:101
  8.0 258.5 %all-gather.9.cloned.1.call-start = ((), (), s32[]{:S(2)}) async-start(), calls=%async_computation.4 | async-start | bytes 10485760 | tf_op jit(solution)/shard_map/all_gather | solution.py:99
  16.6 32.9 %all-to-all-start = ((bf16[4,192,1024]{2,1,0:T(8,128)(2,1)}), bf16[4,192,1024]{2,1,0:T(8,128)(2,1)S(1)}, u32[]{:S(2)}, u32[]{:S(2)}) async-start(bf16[4,192,1024]{2,1,0:T(8,128)(2,1)} %bitcast.6), calls=%async_computation | async-start | bytes 3145728 | tf_op jit(solution)/shard_map/all_to_all | solution.py:65
  20.9 260.7 %all-gather.11.cloned.1.call-start = ((), (), s32[]{:S(2)}) async-start(), calls=%async_computation.5 | async-start | bytes 10485760 | tf_op jit(solution)/shard_map/all_gather | solution.py:127
  55.5 27.7 %collective-permute-start = (bf16[512,1024]{1,0:T(8,128)(2,1)S(1)}, bf16[512,1024]{1,0:T(8,128)(2,1)S(1)}, u32[]{:S(2)}, u32[]{:S(2)}) collective-permute-start(bf16[512,1024]{1,0:T(8,128)(2,1)S(1)} %scatter_custom_fusion.2), channel_id=1, source_target_pairs={{0,1},{1,2},{2,3},{3,4},{4,5},{5,6},{6,7},{7,0},{8,9},{9,10},{10,1... | collective-permute-start | bytes 3145736 | tf_op jit(solution)/shard_map/ppermute | solution.py:88
  83.2 26.8 %collective-permute-start.1 = (bf16[512,1024]{1,0:T(8,128)(2,1)S(1)}, bf16[512,1024]{1,0:T(8,128)(2,1)S(1)}, u32[]{:S(2)}, u32[]{:S(2)}) collective-permute-start(bf16[512,1024]{1,0:T(8,128)(2,1)S(1)} %collective-permute-done), channel_id=1, source_target_pairs={{0,1},{1,2},{2,3},{3,4},{4,5},{5,6},{6,7},{7,0},{8,9},{9,10},{10,1... | collective-permute-start | bytes 3145736 | tf_op jit(solution)/shard_map/ppermute | solution.py:88
  83.2 354.0 %reduce-scatter.2.cloned.1.call-start = ((), (), s32[]{:S(2)}) async-start(), calls=%async_computation.6 | async-start | bytes 9437184 | tf_op jit(solution)/shard_map/reduce_scatter | solution.py:129
  110.0 25.9 %collective-permute-start.2 = (bf16[512,1024]{1,0:T(8,128)(2,1)S(1)}, bf16[512,1024]{1,0:T(8,128)(2,1)S(1)}, u32[]{:S(2)}, u32[]{:S(2)}) collective-permute-start(bf16[512,1024]{1,0:T(8,128)(2,1)S(1)} %collective-permute-done.1), channel_id=1, source_target_pairs={{0,1},{1,2},{2,3},{3,4},{4,5},{5,6},{6,7},{7,0},{8,9},{9,10},{10,1... | collective-permute-start | bytes 3145736 | tf_op jit(solution)/shard_map/ppermute | solution.py:88
  135.9 1.0 copy-start.1
  136.9 25.1 %collective-permute-start.3 = (bf16[512,1024]{1,0:T(8,128)(2,1)S(1)}, bf16[512,1024]{1,0:T(8,128)(2,1)S(1)}, u32[]{:S(2)}, u32[]{:S(2)}) collective-permute-start(bf16[512,1024]{1,0:T(8,128)(2,1)S(1)} %collective-permute-done.2), channel_id=1, source_target_pairs={{0,1},{1,2},{2,3},{3,4},{4,5},{5,6},{6,7},{7,0},{8,9},{9,10},{10,1... | collective-permute-start | bytes 3145736 | tf_op jit(solution)/shard_map/ppermute | solution.py:88
  162.0 1.0 copy-start.3
  163.0 24.2 %collective-permute-start.4 = (bf16[512,1024]{1,0:T(8,128)(2,1)S(1)}, bf16[512,1024]{1,0:T(8,128)(2,1)S(1)}, u32[]{:S(2)}, u32[]{:S(2)}) collective-permute-start(bf16[512,1024]{1,0:T(8,128)(2,1)S(1)} %collective-permute-done.3), channel_id=1, source_target_pairs={{0,1},{1,2},{2,3},{3,4},{4,5},{5,6},{6,7},{7,0},{8,9},{9,10},{10,1... | collective-permute-start | bytes 3145736 | tf_op jit(solution)/shard_map/ppermute | solution.py:88
  187.3 1.0 copy-start.5
  188.2 23.5 %collective-permute-start.5 = (bf16[512,1024]{1,0:T(8,128)(2,1)S(1)}, bf16[512,1024]{1,0:T(8,128)(2,1)}, u32[]{:S(2)}, u32[]{:S(2)}) collective-permute-start(bf16[512,1024]{1,0:T(8,128)(2,1)S(1)} %collective-permute-done.4), channel_id=1, source_target_pairs={{0,1},{1,2},{2,3},{3,4},{4,5},{5,6},{6,7},{7,0},{8,9},{9,10},{10,1... | collective-permute-start | bytes 3145736 | tf_op jit(solution)/shard_map/ppermute | solution.py:88
  211.7 22.8 %collective-permute-start.6 = (bf16[512,1024]{1,0:T(8,128)(2,1)}, bf16[512,1024]{1,0:T(8,128)(2,1)}, u32[]{:S(2)}, u32[]{:S(2)}) collective-permute-start(bf16[512,1024]{1,0:T(8,128)(2,1)} %collective-permute-done.5), channel_id=1, source_target_pairs={{0,1},{1,2},{2,3},{3,4},{4,5},{5,6},{6,7},{7,0},{8,9},{9,10},{10,1... | collective-permute-start | bytes 3145736 | tf_op jit(solution)/shard_map/ppermute | solution.py:88
  211.7 32.3 %copy-start.6 = (bf16[512,1024]{1,0:T(8,128)(2,1)S(1)}, bf16[512,1024]{1,0:T(8,128)(2,1)}, u32[]{:S(2)}) copy-start(bf16[512,1024]{1,0:T(8,128)(2,1)} %copy-done.5) | copy-start | bytes 3145732
  211.7 32.4 %copy-start.4 = (bf16[512,1024]{1,0:T(8,128)(2,1)S(1)}, bf16[512,1024]{1,0:T(8,128)(2,1)}, u32[]{:S(2)}) copy-start(bf16[512,1024]{1,0:T(8,128)(2,1)} %copy-done.3) | copy-start | bytes 3145732
  211.8 32.5 %copy-start.2 = (bf16[512,1024]{1,0:T(8,128)(2,1)S(1)}, bf16[512,1024]{1,0:T(8,128)(2,1)}, u32[]{:S(2)}) copy-start(bf16[512,1024]{1,0:T(8,128)(2,1)} %copy-done.1) | copy-start | bytes 3145732
  239.8 12.4 %copy-start.8 = (f32[8192]{0:T(1024)S(1)}, f32[8192]{0:T(1024)}, u32[]{:S(2)}) copy-start(f32[8192]{0:T(1024)} %param.10) | copy-start | bytes 98308
  244.7 5.7 %copy-start = (bf16[512,16384]{1,0:T(8,128)(2,1)}, bf16[512,16384]{1,0:T(8,128)(2,1)S(1)}, u32[]{:S(2)}) copy-start(bf16[512,16384]{1,0:T(8,128)(2,1)S(1)} %constant_dynamic-update-slice_fusion) | copy-start | bytes 50331652
  266.5 12.4 %copy-start.7 = (f32[512,64]{1,0:T(8,128)S(1)}, f32[512,64]{1,0:T(8,128)}, u32[]{:S(2)}) copy-start(f32[512,64]{1,0:T(8,128)} %get-tuple-element.16) | copy-start | bytes 393220
Sparse Core Ops, SparseCore 0:
  8.9 33.8 all-gather.6
  44.3 21.8 all-gather.4
  67.8 58.2 all-gather.8
  127.5 58.2 all-gather.10
  291.8 145.3 reduce-scatter.1
